TPU v7x, 512 devices: a whole 4x8x8 slice. The times are simulated.
512 devices in a mesh: segment: 8 (over y), rows: 64 (over x, z, core).
Axes of the slice: x: 4, y: 8, z: 8, core: 2. Of those that a mesh axis runs over, the one named last changes fastest.
Arguments:
- incoming: bfloat16 [8, 256, 128, 128], P('segment', 'rows'), may hold values from -6 to 6
- cotangent: bfloat16 [8, 256, 128, 128], P('segment', 'rows'), may hold values from -6 to 6
- main_weight: bfloat16 [8, 3, 3, 128, 128], P('segment'), may hold values from -0.1875 to 0.1875
- second_weight: bfloat16 [8, 3, 3, 128, 128], P('segment'), may hold values from -0.1875 to 0.1875
Outputs:
- output: bfloat16 [8, 256, 128, 128], P('segment', 'rows')
- input_grad: bfloat16 [8, 256, 128, 128], P('segment', 'rows')
- main_grad: float32 [8, 3, 3, 128, 128], P('segment')
- second_grad: float32 [8, 3, 3, 128, 128], P('segment')
All inputs are finite; a program needn't handle non-finite values.
Results may differ from a plain program's by a relative error of at most 0.011.
Values may be sent and summed in bfloat16 or wider, within the bound.
A program may use at most 64 MiB of HBM per device.

v0:
```python
import math

import jax
import jax.numpy as jnp
from jax import lax
from jax.sharding import PartitionSpec as P


def padded_2(block, sides, width):
    for axis, dim in sides:
        count = lax.axis_size(axis)
        forward = [(i, i + 1) for i in range(count - 1)]
        backward = [(target, source) for source, target in forward]
        low = lax.ppermute(
            lax.slice_in_dim(block, block.shape[dim] - width, None, axis=dim), axis, forward
        )
        high = lax.ppermute(lax.slice_in_dim(block, 0, width, axis=dim), axis, backward)
        block = jnp.concatenate([low, block, high], axis=dim)
    return block


def partner(array, axis, apart):
    return lax.ppermute(array, axis, [(i, i ^ 1 << apart) for i in range(lax.axis_size(axis))])


def silu(values):
    return values * jax.nn.sigmoid(values)


def slope(values):
    gate_value = jax.nn.sigmoid(values)
    return gate_value * (1.0 + values * (1.0 - gate_value))


def widen(padded):
    breadth = padded.shape[1]
    widened = jnp.pad(padded, ((0, 0), (1, 1), (0, 0)))
    return jnp.concatenate(
        [widened[:, 0:breadth], widened[:, 1 : breadth + 1], widened[:, 2 : breadth + 2]], axis=-1
    )


def convolve(padded, weight):
    stacked = widen(padded)
    height = padded.shape[0] - 2
    breadth = padded.shape[1]
    inner_dim = stacked.shape[-1]
    summed = jnp.zeros((height * breadth, weight.shape[-1]), jnp.float32)
    for offset in range(3):
        summed = summed + jnp.dot(
            stacked[offset : offset + height].reshape(-1, inner_dim),
            weight[offset].reshape(inner_dim, -1),
            preferred_element_type=jnp.float32,
        )
    return summed.reshape(height, breadth, -1)


def transpose_conv(padded, weight):
    return convolve(padded, jnp.flip(weight, (0, 1)).transpose(0, 1, 3, 2))


def weight_grad(padded, gradient):
    stacked = widen(padded)
    height = gradient.shape[0]
    inner_dim = stacked.shape[-1]
    outer_dim = gradient.shape[-1]
    pieces = []
    for offset in range(3):
        product = lax.dot_general(
            stacked[offset : offset + height].reshape(-1, inner_dim),
            gradient.reshape(-1, outer_dim),
            (((0,), (0,)), ((), ())),
            preferred_element_type=jnp.float32,
        )
        pieces.append(product.reshape(3, -1, outer_dim))
    return jnp.stack(pieces)


def margin(field):
    return padded_2(field, (("rows", 0),), 1)


def mirror(field, top_bit):
    return partner(field, "segment", top_bit)


def body(incoming, cotangent, main_weight, second_weight):
    source = incoming[0]
    upstream = cotangent[0]
    first_kernel = main_weight[0]
    second_kernel = second_weight[0]
    strip_rows, columns, channels = source.shape
    segments = lax.axis_size("segment")
    top_bit = segments.bit_length() - 2
    encoder = lax.axis_index("segment") < segments // 2
    nothing = jnp.zeros((strip_rows, columns, channels), jnp.float32)
    source_rim = margin(source)
    first_pre = convolve(source_rim, first_kernel)
    hidden = silu(first_pre).astype(jnp.bfloat16)
    hidden_rim = margin(hidden)
    encoder_pre = lax.cond(encoder, lambda: convolve(hidden_rim, second_kernel), lambda: nothing)
    skip_rim = margin(mirror(silu(encoder_pre).astype(jnp.bfloat16), top_bit))
    skip_pre = lax.cond(encoder, lambda: nothing, lambda: convolve(skip_rim, second_kernel))
    final_pre = jnp.where(encoder, encoder_pre, first_pre + skip_pre)
    output = silu(final_pre).astype(jnp.bfloat16)
    decoder_grad = (upstream.astype(jnp.float32) * slope(final_pre)).astype(jnp.bfloat16)
    decoder_rim = margin(decoder_grad)
    skip_grad, decoder_input = lax.cond(
        encoder,
        lambda: (nothing, nothing),
        lambda: (
            transpose_conv(decoder_rim, second_kernel),
            transpose_conv(decoder_rim, first_kernel),
        ),
    )
    returned = mirror(skip_grad.astype(jnp.bfloat16), top_bit)
    encoder_grad = (
        (upstream.astype(jnp.float32) + returned.astype(jnp.float32)) * slope(encoder_pre)
    ).astype(jnp.bfloat16)
    encoder_rim = margin(encoder_grad)
    hidden_back = lax.cond(
        encoder, lambda: transpose_conv(encoder_rim, second_kernel), lambda: nothing
    )
    hidden_grad = (hidden_back * slope(first_pre)).astype(jnp.bfloat16)
    hidden_grad_rim = margin(hidden_grad)
    encoder_input = lax.cond(
        encoder, lambda: transpose_conv(hidden_grad_rim, first_kernel), lambda: nothing
    )
    input_grad = jnp.where(encoder, encoder_input, decoder_input).astype(jnp.bfloat16)
    first_terms = weight_grad(source_rim, jnp.where(encoder, hidden_grad, decoder_grad))
    second_terms = weight_grad(
        jnp.where(encoder, hidden_rim, skip_rim), jnp.where(encoder, encoder_grad, decoder_grad)
    )
    first_sum, second_sum = lax.psum((first_terms, second_terms), "rows")
    factor = 1.0 / math.sqrt(strip_rows * lax.axis_size("rows") * columns)
    return (output[None], input_grad[None], (first_sum * factor)[None], (second_sum * factor)[None])


def solution(mesh):
    return jax.shard_map(
        body,
        mesh=mesh,
        in_specs=(
            P("segment", "rows", None, None),
            P("segment", "rows", None, None),
            P("segment", None, None, None, None),
            P("segment", None, None, None, None),
        ),
        out_specs=(
            P("segment", "rows", None, None),
            P("segment", "rows", None, None),
            P("segment", None, None, None, None),
            P("segment", None, None, None, None),
        ),
        check_vma=False,
    )
```

profile of v0, /device:TPU:16, one launch (start us, length us, event | category | flops | bytes accessed | tf_op | source)
XLA Modules:
  0.0 310.3 jit_solution(8175913941270397367)
XLA Ops:
  8.0 1.3 collective-permute-start.1
  9.3 3.0 collective-permute-start
  12.4 1.0 fusion.25
  14.7 1.3 collective-permute-start.3
  16.0 4.5 %collective-permute-start.2 = (bf16[1,128,128]{2,1,0:T(8,128)(2,1)S(1)}, bf16[1,128,128]{2,1,0:T(8,128)(2,1)S(1)}, u32[]{:S(2)}, u32[]{:S(2)}) collective-permute-start(bf16[1,128,128]{2,1,0:T(8,128)(2,1)S(1)} %get-tuple-element.134), channel_id=1, source_target_pairs={{0,1},{1,2},{2,3},{3,4},{4,5},{5,6},{6,7},{7,8},{8,9},{9,10},{10,1... | collective-permute-start | bytes 98312 | tf_op jit(solution)/shard_map/ppermute | solution.py:14
  21.4 3.1 %conditional.5 = (f32[4,128,128]{2,1,0:T(8,128)}, f32[4,128,128]{2,1,0:T(8,128)S(1)}) conditional(s32[]{:T(128)} %convert_element_type.51, () %tuple.44, (bf16[6,128,128]{2,1,0:T(8,128)(2,1)S(1)}, bf16[3,3,128,128]{2,3,1,0:T(8,128)(2,1)S(1)}) %tuple.116), branch_computations={%region_0.1_spmd, %region_1.2_spmd} | conditional | flops 152961024 | bytes 8618000 | solution.py:101
  22.6 1.0 convolution_add_fusion
  23.6 1.0 negate_exponential_fusion
  24.6 1.0 multiply_convert_fusion.2
  25.6 3.6 %collective-permute-start.4 = (bf16[4,128,128]{2,1,0:T(8,128)(2,1)S(1)}, bf16[4,128,128]{2,1,0:T(8,128)(2,1)S(1)}, u32[]{:S(2)}, u32[]{:S(2)}) collective-permute-start(bf16[4,128,128]{2,1,0:T(8,128)(2,1)S(1)} %multiply_convert_fusion.2), channel_id=1, source_target_pairs={{0,256},{64,320},{128,384},{192,448},{256,0},{320,64},{384,128},{4... | collective-permute-start | bytes 393224 | tf_op jit(solution)/shard_map/ppermute | solution.py:23
  29.2 7.3 %collective-permute-done.4 = bf16[4,128,128]{2,1,0:T(8,128)(2,1)S(1)} collective-permute-done((bf16[4,128,128]{2,1,0:T(8,128)(2,1)S(1)}, bf16[4,128,128]{2,1,0:T(8,128)(2,1)S(1)}, u32[]{:S(2)}, u32[]{:S(2)}) %collective-permute-start.4) | collective-permute-done | bytes 131104 | tf_op jit(solution)/shard_map/ppermute | solution.py:23
  36.5 3.1 %collective-permute-start.5 = (bf16[1,128,128]{2,1,0:T(8,128)(2,1)S(1)}, bf16[1,128,128]{2,1,0:T(8,128)(2,1)S(1)}, u32[]{:S(2)}, u32[]{:S(2)}) collective-permute-start(bf16[1,128,128]{2,1,0:T(8,128)(2,1)S(1)} %get-tuple-element.133), channel_id=1, source_target_pairs={{0,1},{1,2},{2,3},{3,4},{4,5},{5,6},{6,7},{7,8},{8,9},{9,10},{10,1... | collective-permute-start | bytes 98312 | tf_op jit(solution)/shard_map/ppermute | solution.py:14
  39.9 0.9 copy.20
  40.8 1.0 copy.19
  41.8 0.9 copy.18
  42.7 1.3 collective-permute-start.6
  44.1 5.4 %collective-permute-done.6 = bf16[1,128,128]{2,1,0:T(8,128)(2,1)S(1)} collective-permute-done((bf16[1,128,128]{2,1,0:T(8,128)(2,1)S(1)}, bf16[1,128,128]{2,1,0:T(8,128)(2,1)S(1)}, u32[]{:S(2)}, u32[]{:S(2)}) %collective-permute-start.6) | collective-permute-done | bytes 32800 | tf_op jit(solution)/shard_map/ppermute | solution.py:17
  50.4 1.1 fusion.1
  51.5 1.3 collective-permute-start.8
  52.8 5.2 %collective-permute-start.7 = (bf16[1,128,128]{2,1,0:T(8,128)(2,1)S(1)}, bf16[1,128,128]{2,1,0:T(8,128)(2,1)S(1)}, u32[]{:S(2)}, u32[]{:S(2)}) collective-permute-start(bf16[1,128,128]{2,1,0:T(8,128)(2,1)S(1)} %get-tuple-element.130), channel_id=1, source_target_pairs={{0,1},{1,2},{2,3},{3,4},{4,5},{5,6},{6,7},{7,8},{8,9},{9,10},{10,1... | collective-permute-start | bytes 98312 | tf_op jit(solution)/shard_map/ppermute | solution.py:14
  60.2 7.4 %collective-permute-start.9 = (bf16[4,128,128]{2,1,0:T(8,128)(2,1)}, bf16[4,128,128]{2,1,0:T(8,128)(2,1)}, u32[]{:S(2)}, u32[]{:S(2)}) collective-permute-start(bf16[4,128,128]{2,1,0:T(8,128)(2,1)} %get-tuple-element.54), channel_id=1, source_target_pairs={{0,256},{64,320},{128,384},{192,448},{256,0},{320,64},{384,128},{4... | collective-permute-start | bytes 393224 | tf_op jit(solution)/shard_map/ppermute | solution.py:23
  68.3 3.0 collective-permute-done.9
  71.2 1.1 broadcast_select_fusion.1
  72.4 1.3 collective-permute-start.11
  73.7 3.9 %collective-permute-start.10 = (bf16[1,128,128]{2,1,0:T(8,128)(2,1)S(1)}, bf16[1,128,128]{2,1,0:T(8,128)(2,1)S(1)}, u32[]{:S(2)}, u32[]{:S(2)}) collective-permute-start(bf16[1,128,128]{2,1,0:T(8,128)(2,1)S(1)} %get-tuple-element.128), channel_id=1, source_target_pairs={{0,1},{1,2},{2,3},{3,4},{4,5},{5,6},{6,7},{7,8},{8,9},{9,10},{10,1... | collective-permute-start | bytes 98312 | tf_op jit(solution)/shard_map/ppermute | solution.py:14
  79.3 1.2 conditional.8
  82.8 0.9 pad_maximum_fusion.6
  83.7 1.3 collective-permute-start.13
  85.0 10.2 %collective-permute-start.12 = (bf16[1,128,128]{2,1,0:T(8,128)(2,1)S(1)}, bf16[1,128,128]{2,1,0:T(8,128)(2,1)S(1)}, u32[]{:S(2)}, u32[]{:S(2)}) collective-permute-start(bf16[1,128,128]{2,1,0:T(8,128)(2,1)S(1)} %get-tuple-element.126), channel_id=1, source_target_pairs={{0,1},{1,2},{2,3},{3,4},{4,5},{5,6},{6,7},{7,8},{8,9},{9,10},{10,1... | collective-permute-start | bytes 98312 | tf_op jit(solution)/shard_map/ppermute | solution.py:14
  96.1 1.2 conditional.9
  98.0 203.1 %all-reduce.10.cloned.1.call-done = (f32[3,3,128,128]{3,2,1,0:T(8,128)}, f32[3,3,128,128]{3,2,1,0:T(8,128)}) async-done(((f32[3,3,128,128]{3,2,1,0:T(8,128)}, f32[3,3,128,128]{3,2,1,0:T(8,128)}), (f32[3,3,128,128]{3,2,1,0:T(8,128)}, f32[3,3,128,128]{3,2,1,0:T(8,128)})) %all-reduce.10.cloned.1.call-update) | async-done | bytes 1179664 | tf_op jit(solution)/shard_map/psum | solution.py:134
  301.1 2.4 multiply_bitcast_fusion
  (101 shorter events, 16.6 us)
Async XLA Ops:
  7.2 6.2 %copy-start.4 = (bf16[1,4,128,128]{3,2,1,0:T(8,128)(2,1)S(1)}, bf16[1,4,128,128]{3,2,1,0:T(8,128)(2,1)}, u32[]{:S(2)}) copy-start(bf16[1,4,128,128]{3,2,1,0:T(8,128)(2,1)} %param.14) | copy-start | bytes 393220
  7.2 293.9 %all-reduce.10.cloned.1.call-start = ((), (), s32[]{:S(2)}) async-start(), calls=%async_computation | async-start | bytes 2359296 | tf_op jit(solution)/shard_map/psum | solution.py:134
  8.0 5.3 %collective-permute-start.1 = (bf16[1,128,128]{2,1,0:T(8,128)(2,1)S(1)}, bf16[1,128,128]{2,1,0:T(8,128)(2,1)S(1)}, u32[]{:S(2)}, u32[]{:S(2)}) collective-permute-start(bf16[1,128,128]{2,1,0:T(8,128)(2,1)S(1)} %get-tuple-element.137), channel_id=1, source_target_pairs={{1,0},{2,1},{3,2},{4,3},{5,4},{6,5},{7,6},{8,7},{9,8},{10,9},{11,1... | collective-permute-start | bytes 98312 | tf_op jit(solution)/shard_map/ppermute | solution.py:17
  9.3 4.1 %collective-permute-start = (bf16[1,128,128]{2,1,0:T(8,128)(2,1)S(1)}, bf16[1,128,128]{2,1,0:T(8,128)(2,1)S(1)}, u32[]{:S(2)}, u32[]{:S(2)}) collective-permute-start(bf16[1,128,128]{2,1,0:T(8,128)(2,1)S(1)} %get-tuple-element.136), channel_id=1, source_target_pairs={{0,1},{1,2},{2,3},{3,4},{4,5},{5,6},{6,7},{7,8},{8,9},{9,10},{10,1... | collective-permute-start | bytes 98312 | tf_op jit(solution)/shard_map/ppermute | solution.py:14
  14.3 6.2 %copy-start.9 = (bf16[1,3,3,128,128]{4,3,2,1,0:T(8,128)(2,1)S(1)}, bf16[1,3,3,128,128]{4,3,2,1,0:T(8,128)(2,1)}, u32[]{:S(2)}) copy-start(bf16[1,3,3,128,128]{4,3,2,1,0:T(8,128)(2,1)} %param.17) | copy-start | bytes 884740
  14.7 6.1 %collective-permute-start.3 = (bf16[1,128,128]{2,1,0:T(8,128)(2,1)S(1)}, bf16[1,128,128]{2,1,0:T(8,128)(2,1)S(1)}, u32[]{:S(2)}, u32[]{:S(2)}) collective-permute-start(bf16[1,128,128]{2,1,0:T(8,128)(2,1)S(1)} %get-tuple-element.135), channel_id=1, source_target_pairs={{1,0},{2,1},{3,2},{4,3},{5,4},{6,5},{7,6},{8,7},{9,8},{10,9},{11,1... | collective-permute-start | bytes 98312 | tf_op jit(solution)/shard_map/ppermute | solution.py:17
  16.0 5.4 %collective-permute-start.2 = (bf16[1,128,128]{2,1,0:T(8,128)(2,1)S(1)}, bf16[1,128,128]{2,1,0:T(8,128)(2,1)S(1)}, u32[]{:S(2)}, u32[]{:S(2)}) collective-permute-start(bf16[1,128,128]{2,1,0:T(8,128)(2,1)S(1)} %get-tuple-element.134), channel_id=1, source_target_pairs={{0,1},{1,2},{2,3},{3,4},{4,5},{5,6},{6,7},{7,8},{8,9},{9,10},{10,1... | collective-permute-start | bytes 98312 | tf_op jit(solution)/shard_map/ppermute | solution.py:14
  24.6 15.1 %copy-start.3 = (bf16[1,3,3,128,128]{4,3,2,1,0:T(8,128)(2,1)S(1)}, bf16[1,3,3,128,128]{4,3,2,1,0:T(8,128)(2,1)}, u32[]{:S(2)}) copy-start(bf16[1,3,3,128,128]{4,3,2,1,0:T(8,128)(2,1)} %param.16) | copy-start | bytes 884740
  25.6 10.9 %collective-permute-start.4 = (bf16[4,128,128]{2,1,0:T(8,128)(2,1)S(1)}, bf16[4,128,128]{2,1,0:T(8,128)(2,1)S(1)}, u32[]{:S(2)}, u32[]{:S(2)}) collective-permute-start(bf16[4,128,128]{2,1,0:T(8,128)(2,1)S(1)} %multiply_convert_fusion.2), channel_id=1, source_target_pairs={{0,256},{64,320},{128,384},{192,448},{256,0},{320,64},{384,128},{4... | collective-permute-start | bytes 393224 | tf_op jit(solution)/shard_map/ppermute | solution.py:23
  36.5 7.5 %collective-permute-start.5 = (bf16[1,128,128]{2,1,0:T(8,128)(2,1)S(1)}, bf16[1,128,128]{2,1,0:T(8,128)(2,1)S(1)}, u32[]{:S(2)}, u32[]{:S(2)}) collective-permute-start(bf16[1,128,128]{2,1,0:T(8,128)(2,1)S(1)} %get-tuple-element.133), channel_id=1, source_target_pairs={{0,1},{1,2},{2,3},{3,4},{4,5},{5,6},{6,7},{7,8},{8,9},{9,10},{10,1... | collective-permute-start | bytes 98312 | tf_op jit(solution)/shard_map/ppermute | solution.py:14
  42.7 6.7 %collective-permute-start.6 = (bf16[1,128,128]{2,1,0:T(8,128)(2,1)S(1)}, bf16[1,128,128]{2,1,0:T(8,128)(2,1)S(1)}, u32[]{:S(2)}, u32[]{:S(2)}) collective-permute-start(bf16[1,128,128]{2,1,0:T(8,128)(2,1)S(1)} %get-tuple-element.132), channel_id=1, source_target_pairs={{1,0},{2,1},{3,2},{4,3},{5,4},{6,5},{7,6},{8,7},{9,8},{10,9},{11,1... | collective-permute-start | bytes 98312 | tf_op jit(solution)/shard_map/ppermute | solution.py:17
  49.5 0.9 copy-start.5
  51.5 6.7 %collective-permute-start.8 = (bf16[1,128,128]{2,1,0:T(8,128)(2,1)S(1)}, bf16[1,128,128]{2,1,0:T(8,128)(2,1)S(1)}, u32[]{:S(2)}, u32[]{:S(2)}) collective-permute-start(bf16[1,128,128]{2,1,0:T(8,128)(2,1)S(1)} %get-tuple-element.131), channel_id=1, source_target_pairs={{1,0},{2,1},{3,2},{4,3},{5,4},{6,5},{7,6},{8,7},{9,8},{10,9},{11,1... | collective-permute-start | bytes 98312 | tf_op jit(solution)/shard_map/ppermute | solution.py:17
  52.8 6.0 %collective-permute-start.7 = (bf16[1,128,128]{2,1,0:T(8,128)(2,1)S(1)}, bf16[1,128,128]{2,1,0:T(8,128)(2,1)S(1)}, u32[]{:S(2)}, u32[]{:S(2)}) collective-permute-start(bf16[1,128,128]{2,1,0:T(8,128)(2,1)S(1)} %get-tuple-element.130), channel_id=1, source_target_pairs={{0,1},{1,2},{2,3},{3,4},{4,5},{5,6},{6,7},{7,8},{8,9},{9,10},{10,1... | collective-permute-start | bytes 98312 | tf_op jit(solution)/shard_map/ppermute | solution.py:14
  59.5 0.6 copy-start.7
  60.2 11.1 %collective-permute-start.9 = (bf16[4,128,128]{2,1,0:T(8,128)(2,1)}, bf16[4,128,128]{2,1,0:T(8,128)(2,1)}, u32[]{:S(2)}, u32[]{:S(2)}) collective-permute-start(bf16[4,128,128]{2,1,0:T(8,128)(2,1)} %get-tuple-element.54), channel_id=1, source_target_pairs={{0,256},{64,320},{128,384},{192,448},{256,0},{320,64},{384,128},{4... | collective-permute-start | bytes 393224 | tf_op jit(solution)/shard_map/ppermute | solution.py:23
  68.1 3.2 %copy-start.6 = (bf16[1,4,128,128]{3,2,1,0:T(8,128)(2,1)S(1)}, bf16[1,4,128,128]{3,2,1,0:T(8,128)(2,1)}, u32[]{:S(2)}) copy-start(bf16[1,4,128,128]{3,2,1,0:T(8,128)(2,1)} %param.15) | copy-start | bytes 393220
  72.4 6.9 %collective-permute-start.11 = (bf16[1,128,128]{2,1,0:T(8,128)(2,1)S(1)}, bf16[1,128,128]{2,1,0:T(8,128)(2,1)S(1)}, u32[]{:S(2)}, u32[]{:S(2)}) collective-permute-start(bf16[1,128,128]{2,1,0:T(8,128)(2,1)S(1)} %get-tuple-element.129), channel_id=1, source_target_pairs={{1,0},{2,1},{3,2},{4,3},{5,4},{6,5},{7,6},{8,7},{9,8},{10,9},{11,1... | collective-permute-start | bytes 98312 | tf_op jit(solution)/shard_map/ppermute | solution.py:17
  73.7 5.6 %collective-permute-start.10 = (bf16[1,128,128]{2,1,0:T(8,128)(2,1)S(1)}, bf16[1,128,128]{2,1,0:T(8,128)(2,1)S(1)}, u32[]{:S(2)}, u32[]{:S(2)}) collective-permute-start(bf16[1,128,128]{2,1,0:T(8,128)(2,1)S(1)} %get-tuple-element.128), channel_id=1, source_target_pairs={{0,1},{1,2},{2,3},{3,4},{4,5},{5,6},{6,7},{7,8},{8,9},{9,10},{10,1... | collective-permute-start | bytes 98312 | tf_op jit(solution)/shard_map/ppermute | solution.py:14
  80.5 1.0 copy-start
  80.7 1.1 copy-start.1
  81.5 1.0 copy-start.2
  83.7 12.2 %collective-permute-start.13 = (bf16[1,128,128]{2,1,0:T(8,128)(2,1)S(1)}, bf16[1,128,128]{2,1,0:T(8,128)(2,1)S(1)}, u32[]{:S(2)}, u32[]{:S(2)}) collective-permute-start(bf16[1,128,128]{2,1,0:T(8,128)(2,1)S(1)} %get-tuple-element.127), channel_id=1, source_target_pairs={{1,0},{2,1},{3,2},{4,3},{5,4},{6,5},{7,6},{8,7},{9,8},{10,9},{11,1... | collective-permute-start | bytes 98312 | tf_op jit(solution)/shard_map/ppermute | solution.py:17
  85.0 11.0 %collective-permute-start.12 = (bf16[1,128,128]{2,1,0:T(8,128)(2,1)S(1)}, bf16[1,128,128]{2,1,0:T(8,128)(2,1)S(1)}, u32[]{:S(2)}, u32[]{:S(2)}) collective-permute-start(bf16[1,128,128]{2,1,0:T(8,128)(2,1)S(1)} %get-tuple-element.126), channel_id=1, source_target_pairs={{0,1},{1,2},{2,3},{3,4},{4,5},{5,6},{6,7},{7,8},{8,9},{9,10},{10,1... | collective-permute-start | bytes 98312 | tf_op jit(solution)/shard_map/ppermute | solution.py:14
  96.1 1.2 copy-start.8
Sparse Core Ops, SparseCore 0:
  83.8 217.1 all-reduce.9
where the time goes:
time: 311 us; the launch traced here: 310 us
  waiting for transfers between devices  220 us (71%)
  starting transfers between devices  48.6 us (16%)
  between operations  14.6 us (5%)
  local copies, waits for them, and re-layouts  10.8 us (3%)
  other arithmetic  10.5 us (3%)
  matrix products  5.43 us (2%)
    psum x1, waiting for transfers between devices, body(): first_sum, second_sum = lax.psum((first_terms, second_terms), 'rows')  203 us
    ppermute x6, starting transfers between devices, padded_2(): lax.ppermute(lax.slice_in_dim(block, block.shape[dim] - width, None, axis...  29.9 us
    ppermute x2, starting transfers between devices, partner(): lax.ppermute(array, axis, [(i, i ^ 1 << apart) for i in range(lax.axis_si...  10.9 us
    ppermute x2, waiting for transfers between devices, partner(): lax.ppermute(array, axis, [(i, i ^ 1 << apart) for i in range(lax.axis_si...  10.3 us
    ppermute x6, starting transfers between devices, padded_2(): lax.ppermute(lax.slice_in_dim(block, 0, width, axis=dim), axis, backward)  7.73 us
  transfers between devices with their start and end apart: 15, of which 7 were waited for; matrix products, arithmetic and copies ran while one was open for 3% of the time, Pallas kernels for 0%

commit v1 on v0

v1 whole, which is shorter than its diff:
```python
import functools
import math

import jax
import jax.numpy as jnp
from jax import lax
from jax.experimental import pallas as pl
from jax.experimental.pallas import tpu as pltpu
from jax.sharding import PartitionSpec as P

BF16 = jnp.bfloat16
F32 = jnp.float32
CORES = 2
Z_SIZE = 8
C = 128
W = 128
STRIP = 4


def silu(values):
    return values * jax.nn.sigmoid(values)


def slope(values):
    gate_value = jax.nn.sigmoid(values)
    return gate_value * (1.0 + values * (1.0 - gate_value))


def shifted(values, by):
    count = values.shape[0]
    column = lax.rem(lax.broadcasted_iota(jnp.int32, values.shape, 0), W)
    edge = 0 if by == 1 else W - 1
    return jnp.where(column == edge, 0.0, pltpu.roll(values, by % count, 0))


def conv_matrix(ref):
    return jnp.concatenate(
        [jnp.concatenate([ref[0, ty, tx] for tx in range(3)], axis=1) for ty in range(3)], axis=0
    )


def transpose_matrix(ref):
    return jnp.concatenate(
        [
            jnp.concatenate([ref[0, 2 - ty, 2 - tx] for ty in range(3)], axis=1)
            for tx in range(3)
        ],
        axis=0,
    )


def convolve(field, matrix, transposed):
    height = field.shape[0] - 2
    stacked = jnp.concatenate([field[t : t + height] for t in range(3)], axis=-1)
    products = lax.dot_general(
        stacked.reshape(height * W, 3 * C),
        matrix,
        (((1,), (1 if transposed else 0,)), ((), ())),
        preferred_element_type=F32,
    )
    return (
        shifted(products[:, :C], 1) + products[:, C : 2 * C] + shifted(products[:, 2 * C :], -1)
    )


def weight_grad(field, gradient, out_ref, index):
    flat = gradient.reshape(STRIP * W, C)
    wide = flat.astype(F32)
    stacked = jnp.concatenate(
        [shifted(wide, -1).astype(BF16), flat, shifted(wide, 1).astype(BF16)], axis=1
    )
    for ty in range(3):
        taps = lax.dot_general(
            field[ty : ty + STRIP].reshape(STRIP * W, C),
            stacked,
            (((0,), (0,)), ((), ())),
            preferred_element_type=F32,
        )
        for tx in range(3):
            out_ref[index, ty * 3 + tx] = taps[:, tx * C : (tx + 1) * C].astype(BF16)


def kernel(
    nx, nz, segments,
    x_ref, g_ref, a_ref, b_ref,
    out_ref, ig_ref, gs_ref,
    xpad, spad, gpad, hpad, dpad, fpre, epre, stage, back,
    mine, from_core, xsend, xrecv, flat_buf, zsend, zrecv, zout, zall, xout, xall, other,
    send, recv,
):
    seg = lax.axis_index("segment")
    row = lax.axis_index("rows")
    rows = nx * nz * CORES
    half = segments // 2
    core = lax.rem(row, CORES)
    z = lax.rem(row // CORES, nz)
    x = row // (CORES * nz)
    encoder = seg < half
    up = (seg, lax.rem(row + rows - 1, rows))
    down = (seg, lax.rem(row + 1, rows))
    across = (lax.rem(seg + half, segments), row)
    pair = (seg, row + 1 - 2 * core)
    first_row = row == 0
    last_row = row == rows - 1

    def x_peer(d):
        return (seg, (lax.rem(x + d, nx) * nz + z) * CORES + core)

    def z_peer(d):
        return (seg, (x * nz + lax.rem(z + d, nz)) * CORES + core)

    used = [0]

    def remote(src, dst, device):
        k = used[0]
        used[0] += 1
        return pltpu.make_async_remote_copy(
            src_ref=src, dst_ref=dst, send_sem=send.at[k], recv_sem=recv.at[k],
            device_id=device, device_id_type=pl.DeviceIdType.MESH,
        )

    partners = [up, down, across]
    partners += [x_peer(d) for d in range(1, nx)] + [z_peer(d) for d in range(1, nz)]
    barrier = pltpu.get_barrier_semaphore()
    for device in partners:
        pl.semaphore_signal(
            barrier, inc=1, device_id=device, device_id_type=pl.DeviceIdType.MESH
        )
    pl.semaphore_wait(barrier, len(partners))

    x_up = remote(x_ref.at[0, 0:2], xpad.at[6:8], up)
    x_down = remote(x_ref.at[0, 2:4], xpad.at[0:2], down)
    g_up = remote(g_ref.at[0, 0:1], gpad.at[5:6], up)
    g_down = remote(g_ref.at[0, 3:4], gpad.at[0:1], down)
    skip_copy = remote(stage, spad.at[2:6], across)
    back_copy = remote(stage, back, across)
    s_up = remote(spad.at[2:4], spad.at[6:8], up)
    s_down = remote(spad.at[4:6], spad.at[0:2], down)

    x_up.start()
    x_down.start()
    xpad[2:6] = x_ref[0]

    @pl.when(jnp.logical_not(encoder))
    def _():
        g_up.start()
        g_down.start()
        gpad[1:5] = g_ref[0]

    def clear(ref, width, top):
        @pl.when(first_row)
        def _():
            ref[0:width] = jnp.zeros((width, W, C), BF16)

        @pl.when(last_row)
        def _():
            ref[top - width : top] = jnp.zeros((width, W, C), BF16)

    x_up.wait()
    x_down.wait()
    clear(xpad, 2, 8)
    fpre[...] = convolve(xpad[...], conv_matrix(a_ref), False)

    @pl.when(encoder)
    def _():
        hpad[...] = silu(fpre[...]).astype(BF16).reshape(6, W, C)
        clear(hpad, 1, 6)
        epre[...] = convolve(hpad[...], conv_matrix(b_ref), False)
        skip = silu(epre[...]).astype(BF16).reshape(4, W, C)
        stage[...] = skip
        skip_copy.start()
        out_ref[0] = skip
        skip_copy.wait_send()
        back_copy.wait_recv()
        total = g_ref[0].astype(F32) + back[...].astype(F32)
        spad[2:6] = (total * slope(epre[...]).reshape(4, W, C)).astype(BF16)
        s_up.start()
        s_down.start()
        weight_grad(hpad[...], spad[2:6], mine, 1)
        s_up.wait()
        s_down.wait()
        clear(spad, 2, 8)
        hidden_back = convolve(spad[...], transpose_matrix(b_ref), True)
        dpad[...] = (hidden_back * slope(fpre[...])).astype(BF16).reshape(6, W, C)
        clear(dpad, 1, 6)

    @pl.when(jnp.logical_not(encoder))
    def _():
        skip_copy.wait_recv()
        s_up.start()
        s_down.start()
        g_up.wait()
        g_down.wait()
        s_up.wait()
        s_down.wait()
        clear(spad, 2, 8)
        fpre[...] += convolve(spad[...], conv_matrix(b_ref), False)
        pre = fpre[...]
        dpad[...] = (gpad[...].astype(F32) * slope(pre).reshape(6, W, C)).astype(BF16)
        clear(dpad, 1, 6)
        stage[...] = convolve(dpad[...], transpose_matrix(b_ref), True).astype(BF16).reshape(
            4, W, C
        )
        back_copy.start()
        out_ref[0] = silu(fpre[W : 5 * W]).astype(BF16).reshape(4, W, C)
        weight_grad(spad[1:7], dpad[1:5], mine, 1)
        back_copy.wait_send()

    weight_grad(xpad[1:7], dpad[1:5], mine, 0)

    swap = remote(mine.at[1 - core], from_core, pair)
    swap.start()
    ig_ref[0] = convolve(dpad[...], transpose_matrix(a_ref), True).astype(BF16).reshape(4, W, C)
    swap.wait()
    part = C // nx
    for k in range(nx):
        rows_k = slice(k * part, (k + 1) * part)
        xsend[k] = (mine[core, :, rows_k].astype(F32) + from_core[:, rows_k].astype(F32)).astype(
            BF16
        )

    copies = [
        remote(xsend.at[lax.rem(x + d, nx)], xrecv.at[d - 1], x_peer(d)) for d in range(1, nx)
    ]
    for copy in copies:
        copy.start()
    for copy in copies:
        copy.wait()
    total = xsend[x].astype(F32)
    for d in range(1, nx):
        total = total + xrecv[d - 1].astype(F32)
    flat_buf[...] = total.reshape(9 * part, C)
    chunk = 9 * part // nz
    for k in range(nz):
        zsend[k] = flat_buf[k * chunk : (k + 1) * chunk].astype(BF16)
    copies = [
        remote(zsend.at[lax.rem(z + d, nz)], zrecv.at[d - 1], z_peer(d)) for d in range(1, nz)
    ]
    for copy in copies:
        copy.start()
    for copy in copies:
        copy.wait()
    total = zsend[z].astype(F32)
    for d in range(1, nz):
        total = total + zrecv[d - 1].astype(F32)
    zout[...] = total.astype(BF16)

    copies = [remote(zout, zall.at[z], z_peer(d)) for d in range(1, nz)]
    for copy in copies:
        copy.start()
    zall[z] = zout[...]
    for copy in copies:
        copy.wait()
    for k in range(nz):
        flat_buf[k * chunk : (k + 1) * chunk] = zall[k].astype(F32)
    xout[...] = flat_buf[...].astype(BF16).reshape(9, part, C)
    copies = [remote(xout, xall.at[x], x_peer(d)) for d in range(1, nx)]
    for copy in copies:
        copy.start()
    forwards = [remote(xout, other.at[x], pair)]
    forwards[0].start()
    xall[x] = xout[...]
    for d in range(1, nx):
        copies[d - 1].wait()
        source = lax.rem(x + nx - d, nx)
        forwards.append(remote(xall.at[source], other.at[source], pair))
        forwards[d].start()
    for k in range(nx):
        gs_ref[core, :, k * part : (k + 1) * part] = xall[k]
    for copy in forwards:
        copy.wait()
    for k in range(nx):
        gs_ref[1 - core, :, k * part : (k + 1) * part] = other[k]


def body(nx, nz, segments, incoming, cotangent, main_weight, second_weight):
    part = C // nx
    chunk = 9 * part // nz
    field = (1, STRIP, W, C)
    copies = 9 + 2 * (nx - 1) + 2 * (nz - 1) + nx
    vmem = pl.BlockSpec(memory_space=pltpu.VMEM)
    output, input_grad, sums = pl.pallas_call(
        functools.partial(kernel, nx, nz, segments),
        out_shape=(
            jax.ShapeDtypeStruct(field, BF16),
            jax.ShapeDtypeStruct(field, BF16),
            jax.ShapeDtypeStruct((2, 9, C, C), BF16),
        ),
        in_specs=[vmem] * 4,
        out_specs=(vmem,) * 3,
        scratch_shapes=[
            pltpu.VMEM((8, W, C), BF16),
            pltpu.VMEM((8, W, C), BF16),
            pltpu.VMEM((6, W, C), BF16),
            pltpu.VMEM((6, W, C), BF16),
            pltpu.VMEM((6, W, C), BF16),
            pltpu.VMEM((6 * W, C), F32),
            pltpu.VMEM((4 * W, C), F32),
            pltpu.VMEM((4, W, C), BF16),
            pltpu.VMEM((4, W, C), BF16),
            pltpu.VMEM((2, 9, C, C), BF16),
            pltpu.VMEM((9, C, C), BF16),
            pltpu.VMEM((nx, 9, part, C), BF16),
            pltpu.VMEM((nx - 1, 9, part, C), BF16),
            pltpu.VMEM((9 * part, C), F32),
            pltpu.VMEM((nz, chunk, C), BF16),
            pltpu.VMEM((nz - 1, chunk, C), BF16),
            pltpu.VMEM((chunk, C), BF16),
            pltpu.VMEM((nz, chunk, C), BF16),
            pltpu.VMEM((9, part, C), BF16),
            pltpu.VMEM((nx, 9, part, C), BF16),
            pltpu.VMEM((nx, 9, part, C), BF16),
            pltpu.SemaphoreType.DMA((copies,)),
            pltpu.SemaphoreType.DMA((copies,)),
        ],
        compiler_params=pltpu.CompilerParams(
            collective_id=0, has_side_effects=True, vmem_limit_bytes=48 * 2**20
        ),
    )(incoming, cotangent, main_weight, second_weight)
    factor = 1.0 / math.sqrt(STRIP * nx * nz * CORES * W)
    grads = (sums.astype(F32) * factor).reshape(2, 1, 3, 3, C, C)
    return output, input_grad, grads[0], grads[1]


def build(mesh, nz):
    segments = mesh.shape["segment"]
    nx = mesh.shape["rows"] // (nz * CORES)
    field = P("segment", "rows", None, None)
    weight = P("segment", None, None, None, None)
    return jax.shard_map(
        functools.partial(body, nx, nz, segments),
        mesh=mesh,
        in_specs=(field, field, weight, weight),
        out_specs=(field, field, weight, weight),
        check_vma=False,
    )


def solution(mesh):
    return build(mesh, Z_SIZE)
```

time: 311 us -> 76.6 us (0.25)
  the two profiles are of different devices: /device:TPU:16 before, /device:TPU:17 now
where the time goes in v1:
time: 76.6 us; the launch traced here: 76.4 us
  Pallas kernels  69.4 us (91%)
  local copies, waits for them, and re-layouts  6.14 us (8%)
    pallas_call x1, Pallas kernels, body(): pl.pallas_call(functools.partial(kernel, nx, nz, segments), out_shape=(ja...  69.4 us
    unnamed x10, local copies, waits for them, and re-layouts  5.03 us

profile of v1, /device:TPU:17, one launch (start us, length us, event | category | flops | bytes accessed | tf_op | source)
XLA Modules:
  0.0 76.4 jit_solution(18427876711174689865)
XLA Ops:
  0.6 0.0 copy-start
  0.6 1.0 %copy-done = bf16[1,3,3,128,128]{4,3,2,1,0:T(8,128)(2,1)S(1)} copy-done((bf16[1,3,3,128,128]{4,3,2,1,0:T(8,128)(2,1)S(1)}, bf16[1,3,3,128,128]{4,3,2,1,0:T(8,128)(2,1)}, u32[]{:S(2)}) %copy-start) | copy-done | bytes 294936
  1.6 0.0 copy-start.1
  1.6 1.0 %copy-done.1 = bf16[1,3,3,128,128]{4,3,2,1,0:T(8,128)(2,1)S(1)} copy-done((bf16[1,3,3,128,128]{4,3,2,1,0:T(8,128)(2,1)S(1)}, bf16[1,3,3,128,128]{4,3,2,1,0:T(8,128)(2,1)}, u32[]{:S(2)}) %copy-start.1) | copy-done | bytes 294936
  2.6 0.0 copy-start.2
  2.6 0.9 %copy-done.2 = bf16[1,4,128,128]{3,2,1,0:T(8,128)(2,1)S(1)} copy-done((bf16[1,4,128,128]{3,2,1,0:T(8,128)(2,1)S(1)}, bf16[1,4,128,128]{3,2,1,0:T(8,128)(2,1)}, u32[]{:S(2)}) %copy-start.2) | copy-done | bytes 131096
  3.5 0.0 copy-start.3
  3.5 0.9 %copy-done.3 = bf16[1,4,128,128]{3,2,1,0:T(8,128)(2,1)S(1)} copy-done((bf16[1,4,128,128]{3,2,1,0:T(8,128)(2,1)S(1)}, bf16[1,4,128,128]{3,2,1,0:T(8,128)(2,1)}, u32[]{:S(2)}) %copy-start.3) | copy-done | bytes 131096
  4.4 69.4 %shard_map.75 = (bf16[1,4,128,128]{3,2,1,0:T(8,128)(2,1)S(1)}, bf16[1,4,128,128]{3,2,1,0:T(8,128)(2,1)S(1)}, bf16[2,9,128,128]{3,2,1,0:T(8,128)(2,1)S(1)}) custom-call(bf16[1,4,128,128]{3,2,1,0:T(8,128)(2,1)S(1)} %copy-done.2, bf16[1,4,128,128]{3,2,1,0:T(8,128)(2,1)S(1)} %copy-done.3, bf16[1,3,3,128,128]{4,3,2,1,0:T(8,128)(2,1)S(1)} %copy-done, ...), custom_call_target="tpu_custom_call" | custom-call | tf_op jit(solution)/shard_map/pallas_call | solution.py:282
  73.8 0.1 convert_multiply_fusion
  73.9 1.1 %fusion = (f32[1,9,128,128]{3,2,1,0:T(8,128)}, f32[1,9,128,128]{3,2,1,0:T(8,128)}) fusion(f32[2,9,128,128]{3,2,1,0:T(8,128)S(1)} %convert_multiply_fusion), kind=kLoop, calls=%fused_computation.1 | loop fusion | bytes 2359296 | tf_op jit(solution)/shard_map/slice | solution.py:322
  75.0 0.7 copy.10
  75.7 0.7 copy.11
Async XLA Ops:
  0.6 1.0 %copy-start = (bf16[1,3,3,128,128]{4,3,2,1,0:T(8,128)(2,1)S(1)}, bf16[1,3,3,128,128]{4,3,2,1,0:T(8,128)(2,1)}, u32[]{:S(2)}) copy-start(bf16[1,3,3,128,128]{4,3,2,1,0:T(8,128)(2,1)} %a_ref.1) | copy-start | bytes 884740
  1.6 1.0 %copy-start.1 = (bf16[1,3,3,128,128]{4,3,2,1,0:T(8,128)(2,1)S(1)}, bf16[1,3,3,128,128]{4,3,2,1,0:T(8,128)(2,1)}, u32[]{:S(2)}) copy-start(bf16[1,3,3,128,128]{4,3,2,1,0:T(8,128)(2,1)} %b_ref.1) | copy-start | bytes 884740
  2.6 0.9 %copy-start.2 = (bf16[1,4,128,128]{3,2,1,0:T(8,128)(2,1)S(1)}, bf16[1,4,128,128]{3,2,1,0:T(8,128)(2,1)}, u32[]{:S(2)}) copy-start(bf16[1,4,128,128]{3,2,1,0:T(8,128)(2,1)} %x_ref.1) | copy-start | bytes 393220
  3.5 0.9 %copy-start.3 = (bf16[1,4,128,128]{3,2,1,0:T(8,128)(2,1)S(1)}, bf16[1,4,128,128]{3,2,1,0:T(8,128)(2,1)}, u32[]{:S(2)}) copy-start(bf16[1,4,128,128]{3,2,1,0:T(8,128)(2,1)} %g_ref.1) | copy-start | bytes 393220

commit v2 on v1

--- a/solution.py
+++ b/solution.py
@@ -15,6 +15,8 @@
 C = 128
 W = 128
 STRIP = 4
+HALF = C // CORES
+VMEM_BYTES = 67_043_328
 
 
 def silu(values):
@@ -77,16 +79,18 @@
             preferred_element_type=F32,
         )
         for tx in range(3):
-            out_ref[index, ty * 3 + tx] = taps[:, tx * C : (tx + 1) * C].astype(BF16)
+            tap = taps[:, tx * C : (tx + 1) * C].astype(BF16)
+            for core in range(CORES):
+                out_ref[index, core, ty * 3 + tx] = tap[core * HALF : (core + 1) * HALF]
 
 
 def kernel(
     nx, nz, segments,
-    x_ref, g_ref, a_ref, b_ref,
-    out_ref, ig_ref, gs_ref,
-    xpad, spad, gpad, hpad, dpad, fpre, epre, stage, back,
+    x_ref, g_ref, a_hbm, b_hbm,
+    out_hbm, ig_hbm, gs_hbm,
+    out_ref, ig_ref, gs_ref, xpad, spad, gpad, hpad, dpad, a_ref, b_ref, fpre, epre, stage, back,
     mine, from_core, xsend, xrecv, flat_buf, zsend, zrecv, zout, zall, xout, xall, other,
-    send, recv,
+    local, send, recv,
 ):
     seg = lax.axis_index("segment")
     row = lax.axis_index("rows")
@@ -121,6 +125,20 @@
 
     partners = [up, down, across]
     partners += [x_peer(d) for d in range(1, nx)] + [z_peer(d) for d in range(1, nz)]
+    loads = [
+        pltpu.make_async_copy(src, dst, local.at[k])
+        for k, (src, dst) in enumerate(
+            [
+                (x_ref.at[0], xpad.at[2:6]),
+                (a_hbm, a_ref),
+                (g_ref.at[0], gpad.at[1:5]),
+                (b_hbm, b_ref),
+            ]
+        )
+    ]
+    for load in loads:
+        load.start()
+
     barrier = pltpu.get_barrier_semaphore()
     for device in partners:
         pl.semaphore_signal(
@@ -137,15 +155,106 @@
     s_up = remote(spad.at[2:4], spad.at[6:8], up)
     s_down = remote(spad.at[4:6], spad.at[0:2], down)
 
+    part = HALF // nx
+    chunk = 9 * part // nz
+
+    class Reduction:
+        def __init__(self, i):
+            self.i = i
+            self.pair = remote(mine.at[i, 1 - core], from_core.at[i], pair)
+            self.x = [
+                remote(xsend.at[i, lax.rem(x + d, nx)], xrecv.at[i, d - 1], x_peer(d))
+                for d in range(1, nx)
+            ]
+            self.z = [
+                remote(zsend.at[i, lax.rem(z + d, nz)], zrecv.at[i, d - 1], z_peer(d))
+                for d in range(1, nz)
+            ]
+            self.z_back = [remote(zout.at[i], zall.at[i, z], z_peer(d)) for d in range(1, nz)]
+            self.x_back = [remote(xout.at[i], xall.at[i, x], x_peer(d)) for d in range(1, nx)]
+            self.over = [remote(xout.at[i], other.at[i, x], pair)]
+            for d in range(1, nx):
+                source = lax.rem(x + nx - d, nx)
+                self.over.append(remote(xall.at[i, source], other.at[i, source], pair))
+
+        def swap(self):
+            self.pair.start()
+
+        def reduce_x(self):
+            i = self.i
+            self.pair.wait()
+            for k in range(nx):
+                at = slice(k * part, (k + 1) * part)
+                own = mine[i, core, :, at].astype(F32)
+                xsend[i, k] = (own + from_core[i, :, at].astype(F32)).astype(BF16)
+            for copy in self.x:
+                copy.start()
+
+        def reduce_z(self):
+            i = self.i
+            for copy in self.x:
+                copy.wait()
+            total = xsend[i, x].astype(F32)
+            for d in range(1, nx):
+                total = total + xrecv[i, d - 1].astype(F32)
+            flat_buf[i] = total.reshape(9 * part, C)
+            for k in range(nz):
+                zsend[i, k] = flat_buf[i, k * chunk : (k + 1) * chunk].astype(BF16)
+            for copy in self.z:
+                copy.start()
+
+        def gather_z(self):
+            i = self.i
+            for copy in self.z:
+                copy.wait()
+            total = zsend[i, z].astype(F32)
+            for d in range(1, nz):
+                total = total + zrecv[i, d - 1].astype(F32)
+            zout[i] = total.astype(BF16)
+            for copy in self.z_back:
+                copy.start()
+            zall[i, z] = zout[i]
+
+        def gather_x(self):
+            i = self.i
+            for copy in self.z_back:
+                copy.wait()
+            for k in range(nz):
+                flat_buf[i, k * chunk : (k + 1) * chunk] = zall[i, k].astype(F32)
+            xout[i] = flat_buf[i].astype(BF16).reshape(9, part, C)
+            for copy in self.x_back:
+                copy.start()
+            self.over[0].start()
+            xall[i, x] = xout[i]
+
+        def gather_core(self):
+            for d in range(1, nx):
+                self.x_back[d - 1].wait()
+                self.over[d].start()
+
+        def finish(self):
+            i = self.i
+            base = core * HALF
+            for k in range(nx):
+                at = pl.ds(pl.multiple_of(base + k * part, part), part)
+                gs_ref[i, :, at] = xall[i, k]
+            base = HALF - base
+            for copy in self.over:
+                copy.wait()
+            for k in range(nx):
+                at = pl.ds(pl.multiple_of(base + k * part, part), part)
+                gs_ref[i, :, at] = other[i, k]
+
+    first = Reduction(0)
+    second = Reduction(1)
+
     x_up.start()
     x_down.start()
-    xpad[2:6] = x_ref[0]
 
     @pl.when(jnp.logical_not(encoder))
     def _():
         g_up.start()
         g_down.start()
-        gpad[1:5] = g_ref[0]
 
     def clear(ref, width, top):
         @pl.when(first_row)
@@ -156,6 +265,8 @@
         def _():
             ref[top - width : top] = jnp.zeros((width, W, C), BF16)
 
+    for load in loads:
+        load.wait()
     x_up.wait()
     x_down.wait()
     clear(xpad, 2, 8)
@@ -169,17 +280,19 @@
         skip = silu(epre[...]).astype(BF16).reshape(4, W, C)
         stage[...] = skip
         skip_copy.start()
-        out_ref[0] = skip
+        out_ref[...] = skip
         skip_copy.wait_send()
         back_copy.wait_recv()
-        total = g_ref[0].astype(F32) + back[...].astype(F32)
+        total = gpad[1:5].astype(F32) + back[...].astype(F32)
         spad[2:6] = (total * slope(epre[...]).reshape(4, W, C)).astype(BF16)
         s_up.start()
         s_down.start()
         weight_grad(hpad[...], spad[2:6], mine, 1)
+        second.swap()
         s_up.wait()
         s_down.wait()
         clear(spad, 2, 8)
+        second.reduce_x()
         hidden_back = convolve(spad[...], transpose_matrix(b_ref), True)
         dpad[...] = (hidden_back * slope(fpre[...])).astype(BF16).reshape(6, W, C)
         clear(dpad, 1, 6)
@@ -202,83 +315,79 @@
             4, W, C
         )
         back_copy.start()
-        out_ref[0] = silu(fpre[W : 5 * W]).astype(BF16).reshape(4, W, C)
+        out_ref[...] = silu(fpre[W : 5 * W]).astype(BF16).reshape(4, W, C)
         weight_grad(spad[1:7], dpad[1:5], mine, 1)
+        second.swap()
         back_copy.wait_send()
+        second.reduce_x()
 
     weight_grad(xpad[1:7], dpad[1:5], mine, 0)
 
-    swap = remote(mine.at[1 - core], from_core, pair)
-    swap.start()
-    ig_ref[0] = convolve(dpad[...], transpose_matrix(a_ref), True).astype(BF16).reshape(4, W, C)
-    swap.wait()
-    part = C // nx
-    for k in range(nx):
-        rows_k = slice(k * part, (k + 1) * part)
-        xsend[k] = (mine[core, :, rows_k].astype(F32) + from_core[:, rows_k].astype(F32)).astype(
-            BF16
-        )
-
-    copies = [
-        remote(xsend.at[lax.rem(x + d, nx)], xrecv.at[d - 1], x_peer(d)) for d in range(1, nx)
+    first.swap()
+    second.reduce_z()
+    store_out = pltpu.make_async_copy(out_ref, out_hbm.at[0], local.at[4])
+    store_out.start()
+    ig_ref[...] = convolve(dpad[...], transpose_matrix(a_ref), True).astype(BF16).reshape(4, W, C)
+    store_ig = pltpu.make_async_copy(ig_ref, ig_hbm.at[0], local.at[5])
+    store_ig.start()
+    first.reduce_x()
+    second.gather_z()
+    first.reduce_z()
+    second.gather_x()
+    first.gather_z()
+    second.gather_core()
+    first.gather_x()
+    first.gather_core()
+    second.finish()
+    store_second = pltpu.make_async_copy(gs_ref.at[1], gs_hbm.at[1], local.at[6])
+    store_second.start()
+    first.finish()
+    store_first = pltpu.make_async_copy(gs_ref.at[0], gs_hbm.at[0], local.at[7])
+    store_first.start()
+    for store in (store_out, store_ig, store_second, store_first):
+        store.wait()
+
+
+def finish_kernel(
+    factor, out_in, ig_in, gs_in, out_hbm, ig_hbm, first_hbm, second_hbm,
+    out_ref, ig_ref, gs_ref, first, second, loaded, stored,
+):
+    loads = [
+        pltpu.make_async_copy(src, dst, loaded.at[k])
+        for k, (src, dst) in enumerate(
+            [
+                (gs_in.at[0], gs_ref.at[0]),
+                (gs_in.at[1], gs_ref.at[1]),
+                (out_in, out_ref),
+                (ig_in, ig_ref),
+            ]
+        )
     ]
-    for copy in copies:
-        copy.start()
-    for copy in copies:
-        copy.wait()
-    total = xsend[x].astype(F32)
-    for d in range(1, nx):
-        total = total + xrecv[d - 1].astype(F32)
-    flat_buf[...] = total.reshape(9 * part, C)
-    chunk = 9 * part // nz
-    for k in range(nz):
-        zsend[k] = flat_buf[k * chunk : (k + 1) * chunk].astype(BF16)
-    copies = [
-        remote(zsend.at[lax.rem(z + d, nz)], zrecv.at[d - 1], z_peer(d)) for d in range(1, nz)
+    stores = [
+        pltpu.make_async_copy(src, dst, stored.at[k])
+        for k, (src, dst) in enumerate(
+            [(first, first_hbm), (second, second_hbm), (out_ref, out_hbm), (ig_ref, ig_hbm)]
+        )
     ]
-    for copy in copies:
-        copy.start()
-    for copy in copies:
-        copy.wait()
-    total = zsend[z].astype(F32)
-    for d in range(1, nz):
-        total = total + zrecv[d - 1].astype(F32)
-    zout[...] = total.astype(BF16)
-
-    copies = [remote(zout, zall.at[z], z_peer(d)) for d in range(1, nz)]
-    for copy in copies:
-        copy.start()
-    zall[z] = zout[...]
-    for copy in copies:
-        copy.wait()
-    for k in range(nz):
-        flat_buf[k * chunk : (k + 1) * chunk] = zall[k].astype(F32)
-    xout[...] = flat_buf[...].astype(BF16).reshape(9, part, C)
-    copies = [remote(xout, xall.at[x], x_peer(d)) for d in range(1, nx)]
-    for copy in copies:
-        copy.start()
-    forwards = [remote(xout, other.at[x], pair)]
-    forwards[0].start()
-    xall[x] = xout[...]
-    for d in range(1, nx):
-        copies[d - 1].wait()
-        source = lax.rem(x + nx - d, nx)
-        forwards.append(remote(xall.at[source], other.at[source], pair))
-        forwards[d].start()
-    for k in range(nx):
-        gs_ref[core, :, k * part : (k + 1) * part] = xall[k]
-    for copy in forwards:
-        copy.wait()
-    for k in range(nx):
-        gs_ref[1 - core, :, k * part : (k + 1) * part] = other[k]
+    for load in loads:
+        load.start()
+    for k, sums in enumerate((first, second)):
+        loads[k].wait()
+        sums[...] = (gs_ref[k].astype(F32) * factor).reshape(1, 3, 3, C, C)
+        stores[k].start()
+    for k in (2, 3):
+        loads[k].wait()
+        stores[k].start()
+    for store in stores:
+        store.wait()
 
 
 def body(nx, nz, segments, incoming, cotangent, main_weight, second_weight):
-    part = C // nx
+    part = HALF // nx
     chunk = 9 * part // nz
     field = (1, STRIP, W, C)
-    copies = 9 + 2 * (nx - 1) + 2 * (nz - 1) + nx
-    vmem = pl.BlockSpec(memory_space=pltpu.VMEM)
+    copies = 8 + 2 * (1 + 2 * (nx - 1) + 2 * (nz - 1) + nx)
+    hbm = pl.BlockSpec(memory_space=pltpu.HBM)
     output, input_grad, sums = pl.pallas_call(
         functools.partial(kernel, nx, nz, segments),
         out_shape=(
@@ -286,40 +395,66 @@
             jax.ShapeDtypeStruct(field, BF16),
             jax.ShapeDtypeStruct((2, 9, C, C), BF16),
         ),
-        in_specs=[vmem] * 4,
-        out_specs=(vmem,) * 3,
+        in_specs=[hbm] * 4,
+        out_specs=(hbm,) * 3,
         scratch_shapes=[
+            pltpu.VMEM((STRIP, W, C), BF16),
+            pltpu.VMEM((STRIP, W, C), BF16),
+            pltpu.VMEM((2, 9, C, C), BF16),
             pltpu.VMEM((8, W, C), BF16),
             pltpu.VMEM((8, W, C), BF16),
             pltpu.VMEM((6, W, C), BF16),
             pltpu.VMEM((6, W, C), BF16),
             pltpu.VMEM((6, W, C), BF16),
+            pltpu.VMEM((1, 3, 3, C, C), BF16),
+            pltpu.VMEM((1, 3, 3, C, C), BF16),
             pltpu.VMEM((6 * W, C), F32),
             pltpu.VMEM((4 * W, C), F32),
             pltpu.VMEM((4, W, C), BF16),
             pltpu.VMEM((4, W, C), BF16),
-            pltpu.VMEM((2, 9, C, C), BF16),
-            pltpu.VMEM((9, C, C), BF16),
-            pltpu.VMEM((nx, 9, part, C), BF16),
-            pltpu.VMEM((nx - 1, 9, part, C), BF16),
-            pltpu.VMEM((9 * part, C), F32),
-            pltpu.VMEM((nz, chunk, C), BF16),
-            pltpu.VMEM((nz - 1, chunk, C), BF16),
-            pltpu.VMEM((chunk, C), BF16),
-            pltpu.VMEM((nz, chunk, C), BF16),
-            pltpu.VMEM((9, part, C), BF16),
-            pltpu.VMEM((nx, 9, part, C), BF16),
-            pltpu.VMEM((nx, 9, part, C), BF16),
+            pltpu.VMEM((2, CORES, 9, HALF, C), BF16),
+            pltpu.VMEM((2, 9, HALF, C), BF16),
+            pltpu.VMEM((2, nx, 9, part, C), BF16),
+            pltpu.VMEM((2, nx - 1, 9, part, C), BF16),
+            pltpu.VMEM((2, 9 * part, C), F32),
+            pltpu.VMEM((2, nz, chunk, C), BF16),
+            pltpu.VMEM((2, nz - 1, chunk, C), BF16),
+            pltpu.VMEM((2, chunk, C), BF16),
+            pltpu.VMEM((2, nz, chunk, C), BF16),
+            pltpu.VMEM((2, 9, part, C), BF16),
+            pltpu.VMEM((2, nx, 9, part, C), BF16),
+            pltpu.VMEM((2, nx, 9, part, C), BF16),
+            pltpu.SemaphoreType.DMA((8,)),
             pltpu.SemaphoreType.DMA((copies,)),
             pltpu.SemaphoreType.DMA((copies,)),
         ],
         compiler_params=pltpu.CompilerParams(
-            collective_id=0, has_side_effects=True, vmem_limit_bytes=48 * 2**20
+            collective_id=0, has_side_effects=True, vmem_limit_bytes=VMEM_BYTES
         ),
     )(incoming, cotangent, main_weight, second_weight)
     factor = 1.0 / math.sqrt(STRIP * nx * nz * CORES * W)
-    grads = (sums.astype(F32) * factor).reshape(2, 1, 3, 3, C, C)
-    return output, input_grad, grads[0], grads[1]
+    weight = (1, 3, 3, C, C)
+    return pl.pallas_call(
+        functools.partial(finish_kernel, factor),
+        out_shape=(
+            jax.ShapeDtypeStruct(field, BF16),
+            jax.ShapeDtypeStruct(field, BF16),
+            jax.ShapeDtypeStruct(weight, F32),
+            jax.ShapeDtypeStruct(weight, F32),
+        ),
+        in_specs=[hbm] * 3,
+        out_specs=(hbm,) * 4,
+        scratch_shapes=[
+            pltpu.VMEM(field, BF16),
+            pltpu.VMEM(field, BF16),
+            pltpu.VMEM((2, 9, C, C), BF16),
+            pltpu.VMEM(weight, F32),
+            pltpu.VMEM(weight, F32),
+            pltpu.SemaphoreType.DMA((4,)),
+            pltpu.SemaphoreType.DMA((4,)),
+        ],
+        compiler_params=pltpu.CompilerParams(vmem_limit_bytes=VMEM_BYTES),
+    )(output, input_grad, sums)
 
 
 def build(mesh, nz):

time: 76.6 us -> 72.1 us (0.941)
  the two profiles are of different devices: /device:TPU:17 before, /device:TPU:9 now
where the time goes in v2:
time: 72.1 us; the launch traced here: 72 us
  Pallas kernels  71.3 us (99%)
    pallas_call x1, Pallas kernels, body(): pl.pallas_call(functools.partial(kernel, nx, nz, segments), out_shape=(ja...  69.2 us
    pallas_call x1, Pallas kernels, body(): pl.pallas_call(functools.partial(finish_kernel, factor), out_shape=(jax.S...  2.16 us

profile of v2, /device:TPU:9, one launch (start us, length us, event | category | flops | bytes accessed | tf_op | source)
XLA Modules:
  0.0 72.0 jit_solution(13420831525050830003)
XLA Ops:
  0.6 69.2 %shard_map.75 = (bf16[1,4,128,128]{3,2,1,0:T(8,128)(2,1)}, bf16[1,4,128,128]{3,2,1,0:T(8,128)(2,1)}, bf16[2,9,128,128]{3,2,1,0:T(8,128)(2,1)}) custom-call(bf16[1,4,128,128]{3,2,1,0:T(8,128)(2,1)} %x_ref.1, bf16[1,4,128,128]{3,2,1,0:T(8,128)(2,1)} %g_ref.1, bf16[1,3,3,128,128]{4,3,2,1,0:T(8,128)(2,1)} %a_hbm.1, bf16[1,3,3,128,128]{4,3,2,1,0:T(8,128)(2,1)} %b_hbm.1), custom_call_target="tpu_custom_call" | custom-call | tf_op jit(solution)/shard_map/pallas_call | solution.py:391
  69.8 2.2 %shard_map.76 = (bf16[1,4,128,128]{3,2,1,0:T(8,128)(2,1)}, bf16[1,4,128,128]{3,2,1,0:T(8,128)(2,1)}, f32[1,3,3,128,128]{4,3,2,1,0:T(8,128)}, f32[1,3,3,128,128]{4,3,2,1,0:T(8,128)}) custom-call(bf16[1,4,128,128]{3,2,1,0:T(8,128)(2,1)} %get-tuple-element.7.out_in, bf16[1,4,128,128]{3,2,1,0:T(8,128)(2,1)} %get-tuple-element.8.ig_in, ...), custom_call_target="tpu_custom_call" | custom-call | tf_op jit(solution)/shard_map/pallas_call | solution.py:437

commit v3 on v2

--- a/solution.py
+++ b/solution.py
@@ -104,6 +104,8 @@
     down = (seg, lax.rem(row + 1, rows))
     across = (lax.rem(seg + half, segments), row)
     pair = (seg, row + 1 - 2 * core)
+    across_up = (across[0], up[1])
+    across_down = (across[0], down[1])
     first_row = row == 0
     last_row = row == rows - 1
 
@@ -123,7 +125,7 @@
             device_id=device, device_id_type=pl.DeviceIdType.MESH,
         )
 
-    partners = [up, down, across]
+    partners = [up, down, across, across_up, across_down]
     partners += [x_peer(d) for d in range(1, nx)] + [z_peer(d) for d in range(1, nz)]
     loads = [
         pltpu.make_async_copy(src, dst, local.at[k])
@@ -131,7 +133,7 @@
             [
                 (x_ref.at[0], xpad.at[2:6]),
                 (a_hbm, a_ref),
-                (g_ref.at[0], gpad.at[1:5]),
+                (g_ref.at[0], gpad.at[2:6]),
                 (b_hbm, b_ref),
             ]
         )
@@ -148,12 +150,20 @@
 
     x_up = remote(x_ref.at[0, 0:2], xpad.at[6:8], up)
     x_down = remote(x_ref.at[0, 2:4], xpad.at[0:2], down)
-    g_up = remote(g_ref.at[0, 0:1], gpad.at[5:6], up)
-    g_down = remote(g_ref.at[0, 3:4], gpad.at[0:1], down)
-    skip_copy = remote(stage, spad.at[2:6], across)
-    back_copy = remote(stage, back, across)
-    s_up = remote(spad.at[2:4], spad.at[6:8], up)
-    s_down = remote(spad.at[4:6], spad.at[0:2], down)
+    g_up = remote(g_ref.at[0, 0:2], gpad.at[6:8], up)
+    g_down = remote(g_ref.at[0, 2:4], gpad.at[0:2], down)
+    e_up = remote(epre.at[2 * W : 4 * W], epre.at[6 * W : 8 * W], up)
+    e_down = remote(epre.at[4 * W : 6 * W], epre.at[0 : 2 * W], down)
+
+    def crossing(field):
+        return (
+            remote(stage, field.at[2:6], across),
+            remote(stage.at[0:2], field.at[6:8], across_up),
+            remote(stage.at[2:4], field.at[0:2], across_down),
+        )
+
+    skip_copies = crossing(spad)
+    back_copies = crossing(back)
 
     part = HALF // nx
     chunk = 9 * part // nz
@@ -251,10 +261,8 @@
     x_up.start()
     x_down.start()
 
-    @pl.when(jnp.logical_not(encoder))
-    def _():
-        g_up.start()
-        g_down.start()
+    g_up.start()
+    g_down.start()
 
     def clear(ref, width, top):
         @pl.when(first_row)
@@ -276,49 +284,54 @@
     def _():
         hpad[...] = silu(fpre[...]).astype(BF16).reshape(6, W, C)
         clear(hpad, 1, 6)
-        epre[...] = convolve(hpad[...], conv_matrix(b_ref), False)
-        skip = silu(epre[...]).astype(BF16).reshape(4, W, C)
+        epre[2 * W : 6 * W] = convolve(hpad[...], conv_matrix(b_ref), False)
+        skip = silu(epre[2 * W : 6 * W]).astype(BF16).reshape(4, W, C)
         stage[...] = skip
-        skip_copy.start()
+        for copy in skip_copies:
+            copy.start()
+        e_up.start()
+        e_down.start()
         out_ref[...] = skip
-        skip_copy.wait_send()
-        back_copy.wait_recv()
-        total = gpad[1:5].astype(F32) + back[...].astype(F32)
-        spad[2:6] = (total * slope(epre[...]).reshape(4, W, C)).astype(BF16)
-        s_up.start()
-        s_down.start()
+        g_up.wait()
+        g_down.wait()
+        e_up.wait()
+        e_down.wait()
+        for copy in skip_copies:
+            copy.wait_send()
+        epre[...] = slope(epre[...])
+        for copy in back_copies:
+            copy.wait_recv()
+        total = gpad[...].astype(F32) + back[...].astype(F32)
+        spad[...] = (total * epre[...].reshape(8, W, C)).astype(BF16)
+        clear(spad, 2, 8)
         weight_grad(hpad[...], spad[2:6], mine, 1)
         second.swap()
-        s_up.wait()
-        s_down.wait()
-        clear(spad, 2, 8)
-        second.reduce_x()
         hidden_back = convolve(spad[...], transpose_matrix(b_ref), True)
         dpad[...] = (hidden_back * slope(fpre[...])).astype(BF16).reshape(6, W, C)
         clear(dpad, 1, 6)
+        second.reduce_x()
 
     @pl.when(jnp.logical_not(encoder))
     def _():
-        skip_copy.wait_recv()
-        s_up.start()
-        s_down.start()
         g_up.wait()
         g_down.wait()
-        s_up.wait()
-        s_down.wait()
+        for copy in skip_copies:
+            copy.wait_recv()
         clear(spad, 2, 8)
         fpre[...] += convolve(spad[...], conv_matrix(b_ref), False)
         pre = fpre[...]
-        dpad[...] = (gpad[...].astype(F32) * slope(pre).reshape(6, W, C)).astype(BF16)
+        dpad[...] = (gpad[1:7].astype(F32) * slope(pre).reshape(6, W, C)).astype(BF16)
         clear(dpad, 1, 6)
         stage[...] = convolve(dpad[...], transpose_matrix(b_ref), True).astype(BF16).reshape(
             4, W, C
         )
-        back_copy.start()
+        for copy in back_copies:
+            copy.start()
         out_ref[...] = silu(fpre[W : 5 * W]).astype(BF16).reshape(4, W, C)
         weight_grad(spad[1:7], dpad[1:5], mine, 1)
         second.swap()
-        back_copy.wait_send()
+        for copy in back_copies:
+            copy.wait_send()
         second.reduce_x()
 
     weight_grad(xpad[1:7], dpad[1:5], mine, 0)
@@ -386,7 +399,7 @@
     part = HALF // nx
     chunk = 9 * part // nz
     field = (1, STRIP, W, C)
-    copies = 8 + 2 * (1 + 2 * (nx - 1) + 2 * (nz - 1) + nx)
+    copies = 12 + 2 * (1 + 2 * (nx - 1) + 2 * (nz - 1) + nx)
     hbm = pl.BlockSpec(memory_space=pltpu.HBM)
     output, input_grad, sums = pl.pallas_call(
         functools.partial(kernel, nx, nz, segments),
@@ -403,15 +416,15 @@
             pltpu.VMEM((2, 9, C, C), BF16),
             pltpu.VMEM((8, W, C), BF16),
             pltpu.VMEM((8, W, C), BF16),
-            pltpu.VMEM((6, W, C), BF16),
+            pltpu.VMEM((8, W, C), BF16),
             pltpu.VMEM((6, W, C), BF16),
             pltpu.VMEM((6, W, C), BF16),
             pltpu.VMEM((1, 3, 3, C, C), BF16),
             pltpu.VMEM((1, 3, 3, C, C), BF16),
             pltpu.VMEM((6 * W, C), F32),
-            pltpu.VMEM((4 * W, C), F32),
+            pltpu.VMEM((8 * W, C), F32),
             pltpu.VMEM((4, W, C), BF16),
-            pltpu.VMEM((4, W, C), BF16),
+            pltpu.VMEM((8, W, C), BF16),
             pltpu.VMEM((2, CORES, 9, HALF, C), BF16),
             pltpu.VMEM((2, 9, HALF, C), BF16),
             pltpu.VMEM((2, nx, 9, part, C), BF16),

time: 72.1 us -> 80.3 us (1.11)
  the two profiles are of different devices: /device:TPU:9 before, /device:TPU:13 now
where the time goes in v3:
time: 80.3 us; the launch traced here: 80.1 us
  Pallas kernels  79.5 us (99%)
    pallas_call x1, Pallas kernels, body(): pl.pallas_call(functools.partial(kernel, nx, nz, segments), out_shape=(ja...  77.3 us
    pallas_call x1, Pallas kernels, body(): pl.pallas_call(functools.partial(finish_kernel, factor), out_shape=(jax.S...  2.16 us

profile of v3, /device:TPU:13, one launch (start us, length us, event | category | flops | bytes accessed | tf_op | source)
XLA Modules:
  0.0 80.1 jit_solution(10355768991688161249)
XLA Ops:
  0.6 77.3 %shard_map.75 = (bf16[1,4,128,128]{3,2,1,0:T(8,128)(2,1)}, bf16[1,4,128,128]{3,2,1,0:T(8,128)(2,1)}, bf16[2,9,128,128]{3,2,1,0:T(8,128)(2,1)}) custom-call(bf16[1,4,128,128]{3,2,1,0:T(8,128)(2,1)} %x_ref.1, bf16[1,4,128,128]{3,2,1,0:T(8,128)(2,1)} %g_ref.1, bf16[1,3,3,128,128]{4,3,2,1,0:T(8,128)(2,1)} %a_hbm.1, bf16[1,3,3,128,128]{4,3,2,1,0:T(8,128)(2,1)} %b_hbm.1), custom_call_target="tpu_custom_call" | custom-call | tf_op jit(solution)/shard_map/pallas_call | solution.py:404
  78.0 2.2 %shard_map.76 = (bf16[1,4,128,128]{3,2,1,0:T(8,128)(2,1)}, bf16[1,4,128,128]{3,2,1,0:T(8,128)(2,1)}, f32[1,3,3,128,128]{4,3,2,1,0:T(8,128)}, f32[1,3,3,128,128]{4,3,2,1,0:T(8,128)}) custom-call(bf16[1,4,128,128]{3,2,1,0:T(8,128)(2,1)} %get-tuple-element.7.out_in, bf16[1,4,128,128]{3,2,1,0:T(8,128)(2,1)} %get-tuple-element.8.ig_in, ...), custom_call_target="tpu_custom_call" | custom-call | tf_op jit(solution)/shard_map/pallas_call | solution.py:450

commit v4 on v2

--- a/solution.py
+++ b/solution.py
@@ -115,6 +115,28 @@
 
     used = [0]
 
+    class Rim:
+        def __init__(self, up_copy, down_copy):
+            self.up = up_copy
+            self.down = down_copy
+
+        def start_up(self):
+            pl.when(jnp.logical_not(first_row))(self.up.start)
+
+        def start_down(self):
+            pl.when(jnp.logical_not(last_row))(self.down.start)
+
+        def wait(self):
+            @pl.when(jnp.logical_not(first_row))
+            def _():
+                self.up.wait_send()
+                self.down.wait_recv()
+
+            @pl.when(jnp.logical_not(last_row))
+            def _():
+                self.down.wait_send()
+                self.up.wait_recv()
+
     def remote(src, dst, device):
         k = used[0]
         used[0] += 1
@@ -146,14 +168,19 @@
         )
     pl.semaphore_wait(barrier, len(partners))
 
-    x_up = remote(x_ref.at[0, 0:2], xpad.at[6:8], up)
-    x_down = remote(x_ref.at[0, 2:4], xpad.at[0:2], down)
-    g_up = remote(g_ref.at[0, 0:1], gpad.at[5:6], up)
-    g_down = remote(g_ref.at[0, 3:4], gpad.at[0:1], down)
-    skip_copy = remote(stage, spad.at[2:6], across)
-    back_copy = remote(stage, back, across)
-    s_up = remote(spad.at[2:4], spad.at[6:8], up)
-    s_down = remote(spad.at[4:6], spad.at[0:2], down)
+    x_rim = Rim(
+        remote(x_ref.at[0, 0:2], xpad.at[6:8], up), remote(x_ref.at[0, 2:4], xpad.at[0:2], down)
+    )
+    g_rim = Rim(
+        remote(g_ref.at[0, 0:1], gpad.at[5:6], up), remote(g_ref.at[0, 3:4], gpad.at[0:1], down)
+    )
+    s_rim = Rim(
+        remote(spad.at[2:4], spad.at[6:8], up), remote(spad.at[4:6], spad.at[0:2], down)
+    )
+    skip_copies = [
+        remote(stage.at[h : h + 2], spad.at[h + 2 : h + 4], across) for h in (0, 2)
+    ]
+    back_copies = [remote(stage.at[h : h + 2], back.at[h : h + 2], across) for h in (0, 2)]
 
     part = HALF // nx
     chunk = 9 * part // nz
@@ -248,13 +275,13 @@
     first = Reduction(0)
     second = Reduction(1)
 
-    x_up.start()
-    x_down.start()
+    x_rim.start_up()
+    x_rim.start_down()
 
     @pl.when(jnp.logical_not(encoder))
     def _():
-        g_up.start()
-        g_down.start()
+        g_rim.start_up()
+        g_rim.start_down()
 
     def clear(ref, width, top):
         @pl.when(first_row)
@@ -267,8 +294,7 @@
 
     for load in loads:
         load.wait()
-    x_up.wait()
-    x_down.wait()
+    x_rim.wait()
     clear(xpad, 2, 8)
     fpre[...] = convolve(xpad[...], conv_matrix(a_ref), False)
 
@@ -276,21 +302,24 @@
     def _():
         hpad[...] = silu(fpre[...]).astype(BF16).reshape(6, W, C)
         clear(hpad, 1, 6)
-        epre[...] = convolve(hpad[...], conv_matrix(b_ref), False)
-        skip = silu(epre[...]).astype(BF16).reshape(4, W, C)
-        stage[...] = skip
-        skip_copy.start()
-        out_ref[...] = skip
-        skip_copy.wait_send()
-        back_copy.wait_recv()
+        matrix = conv_matrix(b_ref)
+        for h in (0, 2):
+            pre = convolve(hpad[h : h + 4], matrix, False)
+            stage[h : h + 2] = silu(pre).astype(BF16).reshape(2, W, C)
+            skip_copies[h // 2].start()
+            epre[h * W : (h + 2) * W] = pre
+        out_ref[...] = stage[...]
+        for copy in skip_copies:
+            copy.wait_send()
+        for copy in back_copies:
+            copy.wait_recv()
         total = gpad[1:5].astype(F32) + back[...].astype(F32)
         spad[2:6] = (total * slope(epre[...]).reshape(4, W, C)).astype(BF16)
-        s_up.start()
-        s_down.start()
+        s_rim.start_up()
+        s_rim.start_down()
         weight_grad(hpad[...], spad[2:6], mine, 1)
         second.swap()
-        s_up.wait()
-        s_down.wait()
+        s_rim.wait()
         clear(spad, 2, 8)
         second.reduce_x()
         hidden_back = convolve(spad[...], transpose_matrix(b_ref), True)
@@ -299,26 +328,27 @@
 
     @pl.when(jnp.logical_not(encoder))
     def _():
-        skip_copy.wait_recv()
-        s_up.start()
-        s_down.start()
-        g_up.wait()
-        g_down.wait()
-        s_up.wait()
-        s_down.wait()
+        skip_copies[0].wait_recv()
+        s_rim.start_up()
+        skip_copies[1].wait_recv()
+        s_rim.start_down()
+        g_rim.wait()
+        s_rim.wait()
         clear(spad, 2, 8)
         fpre[...] += convolve(spad[...], conv_matrix(b_ref), False)
         pre = fpre[...]
         dpad[...] = (gpad[...].astype(F32) * slope(pre).reshape(6, W, C)).astype(BF16)
         clear(dpad, 1, 6)
-        stage[...] = convolve(dpad[...], transpose_matrix(b_ref), True).astype(BF16).reshape(
-            4, W, C
-        )
-        back_copy.start()
+        matrix = transpose_matrix(b_ref)
+        for h in (0, 2):
+            skip_grad = convolve(dpad[h : h + 4], matrix, True)
+            stage[h : h + 2] = skip_grad.astype(BF16).reshape(2, W, C)
+            back_copies[h // 2].start()
         out_ref[...] = silu(fpre[W : 5 * W]).astype(BF16).reshape(4, W, C)
         weight_grad(spad[1:7], dpad[1:5], mine, 1)
         second.swap()
-        back_copy.wait_send()
+        for copy in back_copies:
+            copy.wait_send()
         second.reduce_x()
 
     weight_grad(xpad[1:7], dpad[1:5], mine, 0)
@@ -386,7 +416,7 @@
     part = HALF // nx
     chunk = 9 * part // nz
     field = (1, STRIP, W, C)
-    copies = 8 + 2 * (1 + 2 * (nx - 1) + 2 * (nz - 1) + nx)
+    copies = 10 + 2 * (1 + 2 * (nx - 1) + 2 * (nz - 1) + nx)
     hbm = pl.BlockSpec(memory_space=pltpu.HBM)
     output, input_grad, sums = pl.pallas_call(
         functools.partial(kernel, nx, nz, segments),

time: 72.1 us -> 70.9 us (0.983)
  Pallas kernels: 71.3 us -> 70.1 us
    pallas_call x1, Pallas kernels: 69.2 us -> 68 us  [body(): pl.pallas_call(functools.partial(kernel, nx, nz, segments), out_shape=(ja...]
where the time goes in v4:
time: 70.9 us; the launch traced here: 70.8 us
  Pallas kernels  70.1 us (99%)
    pallas_call x1, Pallas kernels, body(): pl.pallas_call(functools.partial(kernel, nx, nz, segments), out_shape=(ja...  68 us
    pallas_call x1, Pallas kernels, body(): pl.pallas_call(functools.partial(finish_kernel, factor), out_shape=(jax.S...  2.16 us

profile of v4, /device:TPU:9, one launch (start us, length us, event | category | flops | bytes accessed | tf_op | source)
XLA Modules:
  0.0 70.8 jit_solution(10433398036004696252)
XLA Ops:
  0.6 68.0 %shard_map.75 = (bf16[1,4,128,128]{3,2,1,0:T(8,128)(2,1)}, bf16[1,4,128,128]{3,2,1,0:T(8,128)(2,1)}, bf16[2,9,128,128]{3,2,1,0:T(8,128)(2,1)}) custom-call(bf16[1,4,128,128]{3,2,1,0:T(8,128)(2,1)} %x_ref.1, bf16[1,4,128,128]{3,2,1,0:T(8,128)(2,1)} %g_ref.1, bf16[1,3,3,128,128]{4,3,2,1,0:T(8,128)(2,1)} %a_hbm.1, bf16[1,3,3,128,128]{4,3,2,1,0:T(8,128)(2,1)} %b_hbm.1), custom_call_target="tpu_custom_call" | custom-call | tf_op jit(solution)/shard_map/pallas_call | solution.py:421
  68.6 2.2 %shard_map.76 = (bf16[1,4,128,128]{3,2,1,0:T(8,128)(2,1)}, bf16[1,4,128,128]{3,2,1,0:T(8,128)(2,1)}, f32[1,3,3,128,128]{4,3,2,1,0:T(8,128)}, f32[1,3,3,128,128]{4,3,2,1,0:T(8,128)}) custom-call(bf16[1,4,128,128]{3,2,1,0:T(8,128)(2,1)} %get-tuple-element.7.out_in, bf16[1,4,128,128]{3,2,1,0:T(8,128)(2,1)} %get-tuple-element.8.ig_in, ...), custom_call_target="tpu_custom_call" | custom-call | tf_op jit(solution)/shard_map/pallas_call | solution.py:467

commit v5 on v4

--- a/solution.py
+++ b/solution.py
@@ -355,18 +355,18 @@
 
     first.swap()
     second.reduce_z()
+    first.reduce_x()
     store_out = pltpu.make_async_copy(out_ref, out_hbm.at[0], local.at[4])
     store_out.start()
     ig_ref[...] = convolve(dpad[...], transpose_matrix(a_ref), True).astype(BF16).reshape(4, W, C)
     store_ig = pltpu.make_async_copy(ig_ref, ig_hbm.at[0], local.at[5])
     store_ig.start()
-    first.reduce_x()
+    first.reduce_z()
     second.gather_z()
-    first.reduce_z()
+    first.gather_z()
     second.gather_x()
-    first.gather_z()
+    first.gather_x()
     second.gather_core()
-    first.gather_x()
     first.gather_core()
     second.finish()
     store_second = pltpu.make_async_copy(gs_ref.at[1], gs_hbm.at[1], local.at[6])

time: 70.9 us -> 70.1 us (0.989)
  Pallas kernels: 70.1 us -> 69.3 us
    pallas_call x1, Pallas kernels: 68 us -> 67.1 us  [body(): pl.pallas_call(functools.partial(kernel, nx, nz, segments), out_shape=(ja...]
where the time goes in v5:
time: 70.1 us; the launch traced here: 69.9 us
  Pallas kernels  69.3 us (99%)
    pallas_call x1, Pallas kernels, body(): pl.pallas_call(functools.partial(kernel, nx, nz, segments), out_shape=(ja...  67.1 us
    pallas_call x1, Pallas kernels, body(): pl.pallas_call(functools.partial(finish_kernel, factor), out_shape=(jax.S...  2.16 us

profile of v5, /device:TPU:9, one launch (start us, length us, event | category | flops | bytes accessed | tf_op | source)
XLA Modules:
  0.0 69.9 jit_solution(12984214184935345231)
XLA Ops:
  0.6 67.1 %shard_map.75 = (bf16[1,4,128,128]{3,2,1,0:T(8,128)(2,1)}, bf16[1,4,128,128]{3,2,1,0:T(8,128)(2,1)}, bf16[2,9,128,128]{3,2,1,0:T(8,128)(2,1)}) custom-call(bf16[1,4,128,128]{3,2,1,0:T(8,128)(2,1)} %x_ref.1, bf16[1,4,128,128]{3,2,1,0:T(8,128)(2,1)} %g_ref.1, bf16[1,3,3,128,128]{4,3,2,1,0:T(8,128)(2,1)} %a_hbm.1, bf16[1,3,3,128,128]{4,3,2,1,0:T(8,128)(2,1)} %b_hbm.1), custom_call_target="tpu_custom_call" | custom-call | tf_op jit(solution)/shard_map/pallas_call | solution.py:421
  67.8 2.2 %shard_map.76 = (bf16[1,4,128,128]{3,2,1,0:T(8,128)(2,1)}, bf16[1,4,128,128]{3,2,1,0:T(8,128)(2,1)}, f32[1,3,3,128,128]{4,3,2,1,0:T(8,128)}, f32[1,3,3,128,128]{4,3,2,1,0:T(8,128)}) custom-call(bf16[1,4,128,128]{3,2,1,0:T(8,128)(2,1)} %get-tuple-element.7.out_in, bf16[1,4,128,128]{3,2,1,0:T(8,128)(2,1)} %get-tuple-element.8.ig_in, ...), custom_call_target="tpu_custom_call" | custom-call | tf_op jit(solution)/shard_map/pallas_call | solution.py:467

commit v6 on v5

--- a/solution.py
+++ b/solution.py
@@ -214,7 +214,7 @@
                 at = slice(k * part, (k + 1) * part)
                 own = mine[i, core, :, at].astype(F32)
                 xsend[i, k] = (own + from_core[i, :, at].astype(F32)).astype(BF16)
-            for copy in self.x:
+            for copy in farthest_first(self.x):
                 copy.start()
 
         def reduce_z(self):
@@ -227,7 +227,7 @@
             flat_buf[i] = total.reshape(9 * part, C)
             for k in range(nz):
                 zsend[i, k] = flat_buf[i, k * chunk : (k + 1) * chunk].astype(BF16)
-            for copy in self.z:
+            for copy in farthest_first(self.z):
                 copy.start()
 
         def gather_z(self):
@@ -238,7 +238,7 @@
             for d in range(1, nz):
                 total = total + zrecv[i, d - 1].astype(F32)
             zout[i] = total.astype(BF16)
-            for copy in self.z_back:
+            for copy in farthest_first(self.z_back):
                 copy.start()
             zall[i, z] = zout[i]
 
@@ -249,13 +249,13 @@
             for k in range(nz):
                 flat_buf[i, k * chunk : (k + 1) * chunk] = zall[i, k].astype(F32)
             xout[i] = flat_buf[i].astype(BF16).reshape(9, part, C)
-            for copy in self.x_back:
+            for copy in farthest_first(self.x_back):
                 copy.start()
             self.over[0].start()
             xall[i, x] = xout[i]
 
         def gather_core(self):
-            for d in range(1, nx):
+            for d in sorted(range(1, nx), key=lambda d: min(d, nx - d)):
                 self.x_back[d - 1].wait()
                 self.over[d].start()
 
@@ -376,6 +376,11 @@
     store_first.start()
     for store in (store_out, store_ig, store_second, store_first):
         store.wait()
+
+
+def farthest_first(copies):
+    count = len(copies) + 1
+    return [copies[d - 1] for d in sorted(range(1, count), key=lambda d: -min(d, count - d))]
 
 
 def finish_kernel(

time: 70.1 us -> 69.1 us (0.986)
  Pallas kernels: 69.3 us -> 68.3 us
    pallas_call x1, Pallas kernels: 67.1 us -> 66.1 us  [body(): pl.pallas_call(functools.partial(kernel, nx, nz, segments), out_shape=(ja...]
where the time goes in v6:
time: 69.1 us; the launch traced here: 68.9 us
  Pallas kernels  68.3 us (99%)
    pallas_call x1, Pallas kernels, body(): pl.pallas_call(functools.partial(kernel, nx, nz, segments), out_shape=(ja...  66.1 us
    pallas_call x1, Pallas kernels, body(): pl.pallas_call(functools.partial(finish_kernel, factor), out_shape=(jax.S...  2.16 us

profile of v6, /device:TPU:9, one launch (start us, length us, event | category | flops | bytes accessed | tf_op | source)
XLA Modules:
  0.0 68.9 jit_solution(5656876227830231598)
XLA Ops:
  0.6 66.1 %shard_map.75 = (bf16[1,4,128,128]{3,2,1,0:T(8,128)(2,1)}, bf16[1,4,128,128]{3,2,1,0:T(8,128)(2,1)}, bf16[2,9,128,128]{3,2,1,0:T(8,128)(2,1)}) custom-call(bf16[1,4,128,128]{3,2,1,0:T(8,128)(2,1)} %x_ref.1, bf16[1,4,128,128]{3,2,1,0:T(8,128)(2,1)} %g_ref.1, bf16[1,3,3,128,128]{4,3,2,1,0:T(8,128)(2,1)} %a_hbm.1, bf16[1,3,3,128,128]{4,3,2,1,0:T(8,128)(2,1)} %b_hbm.1), custom_call_target="tpu_custom_call" | custom-call | tf_op jit(solution)/shard_map/pallas_call | solution.py:426
  66.7 2.2 %shard_map.76 = (bf16[1,4,128,128]{3,2,1,0:T(8,128)(2,1)}, bf16[1,4,128,128]{3,2,1,0:T(8,128)(2,1)}, f32[1,3,3,128,128]{4,3,2,1,0:T(8,128)}, f32[1,3,3,128,128]{4,3,2,1,0:T(8,128)}) custom-call(bf16[1,4,128,128]{3,2,1,0:T(8,128)(2,1)} %get-tuple-element.7.out_in, bf16[1,4,128,128]{3,2,1,0:T(8,128)(2,1)} %get-tuple-element.8.ig_in, ...), custom_call_target="tpu_custom_call" | custom-call | tf_op jit(solution)/shard_map/pallas_call | solution.py:472
